TPU v7x, 32 devices: a whole 2x2x4 slice. The times are simulated.
32 devices in a mesh: row: 2 (over x), col: 16 (over z, y, core).
Axes of the slice: x: 2, y: 2, z: 4, core: 2. Of those that a mesh axis runs over, the one named last changes fastest.
Arguments:
- tile_values: float32 [2, 16, 64, 128, 128], P('row', 'col'), may hold values from -0.21875 to 0.21875
- tile_rows: int32 [2, 16, 64], P('row', 'col'), may hold values from 0 to 159, as said below
- tile_cols: int32 [2, 16, 64], P('row', 'col'), may hold values from 0 to 23
- x_start: float32 [384, 128], P('col', 'row'), may hold values from -6 to 6
- z_start: float32 [320, 128], P('row'), may hold values from -6 to 6
- y_start: float32 [320, 128], P('row'), may hold values from -3 to 3
- lower_bound: float32 [320, 128], P('row'), may hold values from -1.5 to -0.1
- upper_bound: float32 [320, 128], P('row'), may hold values from 0.1 to 1.5
- cost_diag: float32 [384, 128], P('col', 'row'), may hold values from 0.1 to 10
- linear: float32 [384, 128], P('col', 'row'), may hold values from -6 to 6
- penalty: float32 [1], replicated, may hold values from 0.3 to 3
- proximal: float32 [1], replicated, may hold values from 0.1 to 1
- relaxation: float32 [1], replicated, may hold values from 1.2 to 1.8
Outputs:
- x_next: float32 [384, 128], P('col', 'row')
- z_next: float32 [320, 128], P('row')
- y_next: float32 [320, 128], P('row')
Inputs may be any that keep to these rules, and one draw needn't show every extreme that they name: On each device the 64 pairs (tile_rows, tile_cols) are distinct.
All inputs are finite; a program needn't handle non-finite values.
Results may differ from a plain program's by a relative error of at most 0.0002.
Values sent between devices are 32-bit elements; how exact they have to be, the bound alone decides.
No kernel may reach another device: no remote copies, remote signals or barrier semaphores. Data moves between devices by JAX's collectives and lax.ppermute only.
A program may use at most 64 MiB of HBM per device.

v0:
```python
import jax
import jax.numpy as jnp
from jax import lax
from jax.sharding import PartitionSpec as P

ADMM_ITERS = 2
HIGH = lax.Precision.HIGHEST


def shards(
    tile_values,
    tile_rows,
    tile_cols,
    x_start,
    z_start,
    y_start,
    lower_bound,
    upper_bound,
    cost_diag,
    linear,
    penalty,
    proximal,
    relaxation,
):
    order_size = tile_values.shape[3]
    flat_tiles = tile_values.reshape(-1, order_size, order_size)
    row_index = tile_rows.reshape(-1)
    col_index = tile_cols.reshape(-1)
    count_tiles = row_index.shape[0]
    block_rows = z_start.shape[0]
    block_cols = x_start.shape[0]
    row_table = (
        lax.broadcasted_iota(jnp.int32, (block_rows, count_tiles), 0) == row_index[None, :]
    ).astype(jnp.float32)
    col_table = (
        lax.broadcasted_iota(jnp.int32, (block_cols, count_tiles), 0) == col_index[None, :]
    ).astype(jnp.float32)
    rho_value = penalty[0]
    sigma_value = proximal[0]
    relax_value = relaxation[0]
    empty_rows = jnp.zeros((block_rows, order_size), jnp.float32)

    def forward_terms(segment):
        picked = jnp.take(segment, col_index, axis=0)
        products = jnp.einsum("kij,kj->ki", flat_tiles, picked, precision=HIGH)
        return jnp.dot(row_table, products, precision=HIGH)

    def apply_forward(vector):
        local_part = forward_terms(lax.all_gather(vector, "row", axis=1, tiled=True))
        return lax.psum(local_part, "col")

    def apply_backward(weights_rows):
        picked = jnp.take(weights_rows, row_index, axis=0)
        products = jnp.einsum("kij,ki->kj", flat_tiles, picked, precision=HIGH)
        local_part = jnp.dot(col_table, products, precision=HIGH)
        return lax.psum_scatter(local_part, "row", scatter_dimension=1, tiled=True)

    def global_totals(values):
        stacked = jnp.stack([jnp.sum(value) for value in values])
        return lax.psum(stacked, ("row", "col"))

    x_now, diag_now, linear_now = (x_start, cost_diag, linear)
    z_now, y_now = (z_start, y_start)
    image_now = empty_rows
    for outer_round in range(ADMM_ITERS):
        if outer_round == 0:
            image_now = apply_forward(x_now)
        target = rho_value * z_now - y_now - rho_value * image_now
        residual = -linear_now - diag_now * x_now + apply_backward(target)
        guess = x_now
        direction = residual
        image_sum = image_now
        norm_now = jnp.float32(1.0)
        norm_now = global_totals([residual * residual])[0]
        pushed = apply_forward(direction)
        applied = (diag_now + sigma_value) * direction + rho_value * apply_backward(pushed)
        curvature = global_totals([direction * applied])[0]
        step_length = norm_now / curvature
        guess = guess + step_length * direction
        image_sum = image_sum + step_length * pushed
        residual = residual - step_length * applied
        image_now = relax_value * image_sum + (1.0 - relax_value) * image_now
        x_now = relax_value * guess + (1.0 - relax_value) * x_now
        mixed = relax_value * image_sum + (1.0 - relax_value) * z_now
        z_fresh = jnp.minimum(jnp.maximum(mixed + y_now / rho_value, lower_bound), upper_bound)
        y_now = y_now + rho_value * (mixed - z_fresh)
        z_now = z_fresh
    return (x_now, z_now, y_now)


def solution(mesh):
    placed = (
        P("row", "col", None, None, None),
        P("row", "col", None),
        P("row", "col", None),
        P("col", "row"),
        P("row", None),
        P("row", None),
        P("row", None),
        P("row", None),
        P("col", "row"),
        P("col", "row"),
        P(),
        P(),
        P(),
    )
    return jax.shard_map(
        shards,
        mesh=mesh,
        in_specs=placed,
        out_specs=(P("col", "row"), P("row", None), P("row", None)),
        check_vma=False,
    )
```

profile of v0, /device:TPU:0, one launch (start us, length us, event | category | flops | bytes accessed | tf_op | source)
XLA Modules:
  0.0 485.3 jit_solution(160176400009086084)
XLA Ops:
  7.2 0.7 compare_select_fusion.1
  7.9 0.7 compare_and_fusion.1
  8.6 5.6 %all-gather = f32[2,64,24]{1,2,0:T(8,128)S(1)} all-gather(f32[1,64,24]{1,2,0:T(8,128)} %bitcast.128), channel_id=1, replica_groups=mesh['row'=2,'col'=16] {'row'}, dimensions={0}, use_global_device_ids=true | all-gather | bytes 18432 | tf_op jit(solution)/shard_map/all_gather | solution.py:49
  14.2 0.1 reshape.90
  14.3 0.6 gather_fusion
  14.9 0.1 broadcast_select_fusion.6
  15.0 8.3 %fusion.12 = f32[64,1,128]{2,1,0:T(1,128)S(1)} fusion(f32[64,128,1]{1,2,0:T(1,128)S(1)} %bitcast.138, f32[1,1,64,128,128]{4,3,2,1,0:T(8,128)} %param.17), kind=kOutput, calls=%fused_computation.19 | convolution fusion | flops 12582912 | bytes 4259840 | tf_op jit(solution)/shard_map/kij,kj->ki/dot_general | solution.py:45
  23.3 0.8 fusion.16
  24.9 87.9 %all-reduce.6.cloned.1.call-done = f32[160,128]{1,0:T(8,128)} async-done(((f32[160,128]{1,0:T(8,128)}), f32[160,128]{1,0:T(8,128)}) %all-reduce.6.cloned.1.call-update) | async-done | bytes 81936 | tf_op jit(solution)/shard_map/psum | solution.py:50
  112.9 0.9 multiply_subtract_fusion.1
  113.8 0.6 gather_fusion.1
  114.4 5.3 %fusion.10 = f32[64,1,128]{2,1,0:T(1,128)S(1)} fusion(f32[64,128,1]{1,2,0:T(1,128)S(1)} %bitcast.139, f32[1,1,64,128,128]{4,3,2,1,0:T(8,128)} %param.17), kind=kOutput, calls=%fused_computation.17 | convolution fusion | flops 12582912 | bytes 4259840 | tf_op jit(solution)/shard_map/kij,ki->kj/dot_general | solution.py:54
  119.7 0.9 convolution_bitcast_fusion.3
  120.7 11.1 %reduce-scatter.13.cloned.1.call-done = f32[64,24]{1,0:T(8,128)} async-done(((f32[128,24]{1,0:T(8,128)}), f32[64,24]{1,0:T(8,128)}) %reduce-scatter.13.cloned.1.call-update) | async-done | bytes 6160
  131.8 0.8 copy.38
  132.6 4.4 all-gather.1
  137.0 0.1 reshape.92
  137.1 0.6 gather_fusion.2
  137.8 8.4 %fusion.8 = f32[64,1,128]{2,1,0:T(1,128)S(1)} fusion(f32[64,128,1]{1,2,0:T(1,128)S(1)} %bitcast.140, f32[1,1,64,128,128]{4,3,2,1,0:T(8,128)} %param.17), kind=kOutput, calls=%fused_computation.15 | convolution fusion | flops 12582912 | bytes 4259840 | tf_op jit(solution)/shard_map/kij,kj->ki/dot_general | solution.py:45
  146.2 0.8 fusion.15
  147.1 87.0 %all-reduce.8.cloned.1.call-done = f32[160,128]{1,0:T(8,128)} async-done(((f32[160,128]{1,0:T(8,128)}), f32[160,128]{1,0:T(8,128)}) %all-reduce.8.cloned.1.call-update) | async-done | bytes 81936 | tf_op jit(solution)/shard_map/psum | solution.py:50
  234.0 1.6 gather_fusion.3
  235.7 5.3 %fusion.6 = f32[64,1,128]{2,1,0:T(1,128)S(1)} fusion(f32[64,128,1]{1,2,0:T(1,128)S(1)} %bitcast.141, f32[1,1,64,128,128]{4,3,2,1,0:T(8,128)} %param.17), kind=kOutput, calls=%fused_computation.13 | convolution fusion | flops 12582912 | bytes 4259840 | tf_op jit(solution)/shard_map/kij,ki->kj/dot_general | solution.py:54
  240.9 0.9 convolution_bitcast_fusion.2
  243.2 9.8 %reduce-scatter.15.cloned.1.call-done = f32[64,24]{1,0:T(8,128)} async-done(((f32[128,24]{1,0:T(8,128)}), f32[64,24]{1,0:T(8,128)}) %reduce-scatter.15.cloned.1.call-update) | async-done | bytes 6160
  253.0 0.8 copy.40
  253.8 0.6 multiply_reduce_fusion.2
  254.4 39.7 %all-reduce.1 = (f32[1]{0:T(128)}, f32[1]{0:T(128)}) all-reduce(f32[1]{0:T(128)} %bitcast.16, f32[1]{0:T(128)} %bitcast.29), channel_id=1, replica_groups=mesh['row'=2,'col'=16] {'row','col'}, use_global_device_ids=true, to_apply=%region_3.6 | all-reduce | flops 2 | bytes 16 | tf_op jit(solution)/shard_map/psum | solution.py:60
  295.6 0.6 gather_fusion.4
  296.3 5.3 %fusion.4 = f32[64,1,128]{2,1,0:T(1,128)S(1)} fusion(f32[64,128,1]{1,2,0:T(1,128)S(1)} %bitcast.142, f32[1,1,64,128,128]{4,3,2,1,0:T(8,128)} %param.17), kind=kOutput, calls=%fused_computation.11 | convolution fusion | flops 12582912 | bytes 4259840 | tf_op jit(solution)/shard_map/kij,ki->kj/dot_general | solution.py:54
  301.5 0.9 convolution_bitcast_fusion.1
  302.5 11.1 %reduce-scatter.17.cloned.1.call-done = f32[64,24]{1,0:T(8,128)} async-done(((f32[128,24]{1,0:T(8,128)}), f32[64,24]{1,0:T(8,128)}) %reduce-scatter.17.cloned.1.call-update) | async-done | bytes 6160
  313.6 0.8 copy.42
  314.4 4.4 all-gather.2
  318.8 0.1 reshape.94
  318.9 0.6 gather_fusion.5
  319.6 8.3 %fusion.2 = f32[64,1,128]{2,1,0:T(1,128)S(1)} fusion(f32[64,128,1]{1,2,0:T(1,128)S(1)} %bitcast.136, f32[1,1,64,128,128]{4,3,2,1,0:T(8,128)} %param.17), kind=kOutput, calls=%fused_computation.9 | convolution fusion | flops 12582912 | bytes 4259840 | tf_op jit(solution)/shard_map/kij,kj->ki/dot_general | solution.py:45
  327.9 0.8 fusion.14
  328.8 87.0 %all-reduce.10.cloned.1.call-done = f32[160,128]{1,0:T(8,128)} async-done(((f32[160,128]{1,0:T(8,128)}), f32[160,128]{1,0:T(8,128)}) %all-reduce.10.cloned.1.call-update) | async-done | bytes 81936 | tf_op jit(solution)/shard_map/psum | solution.py:50
  415.8 1.6 gather_fusion.6
  417.4 5.3 %fusion = f32[64,1,128]{2,1,0:T(1,128)S(1)} fusion(f32[64,128,1]{1,2,0:T(1,128)S(1)} %bitcast.137, f32[1,1,64,128,128]{4,3,2,1,0:T(8,128)} %param.17), kind=kOutput, calls=%fused_computation.7 | convolution fusion | flops 12582912 | bytes 4259840 | tf_op jit(solution)/shard_map/kij,ki->kj/dot_general | solution.py:54
  422.7 0.9 convolution_bitcast_fusion
  423.6 11.1 %reduce-scatter.19.cloned.1.call-done = f32[64,24]{1,0:T(8,128)} async-done(((f32[128,24]{1,0:T(8,128)}), f32[64,24]{1,0:T(8,128)}) %reduce-scatter.19.cloned.1.call-update) | async-done | bytes 6160
  434.8 0.8 copy.44
  435.6 0.6 multiply_reduce_fusion
  436.2 39.5 %all-reduce = (f32[1]{0:T(128)}, f32[1]{0:T(128)}) all-reduce(f32[1]{0:T(128)} %bitcast.35, f32[1]{0:T(128)} %bitcast.47), channel_id=1, replica_groups=mesh['row'=2,'col'=16] {'row','col'}, use_global_device_ids=true, to_apply=%region_10.13 | all-reduce | flops 2 | bytes 16 | tf_op jit(solution)/shard_map/psum | solution.py:60
  477.1 0.6 multiply_add_fusion.5
  477.7 0.7 multiply_add_fusion
  (54 shorter events, 1.1 us)
Async XLA Ops:
  7.2 16.2 %copy-start.11 = (s32[1,1,64]{2,1,0:T(1,128)S(1)}, s32[1,1,64]{2,1,0:T(1,128)}, u32[]{:S(2)}) copy-start(s32[1,1,64]{2,1,0:T(1,128)} %param.18) | copy-start | bytes 772
  7.2 105.7 %copy-start.3 = (f32[160,128]{1,0:T(8,128)S(1)}, f32[160,128]{1,0:T(8,128)}, u32[]{:S(2)}) copy-start(f32[160,128]{1,0:T(8,128)} %param.22) | copy-start | bytes 245764
  7.2 105.7 %copy-start.4 = (f32[160,128]{1,0:T(8,128)S(1)}, f32[160,128]{1,0:T(8,128)}, u32[]{:S(2)}) copy-start(f32[160,128]{1,0:T(8,128)} %param.21) | copy-start | bytes 245764
  7.2 105.7 %all-reduce.6.cloned.1.call-start = ((), (), s32[]{:S(2)}) async-start(), calls=%async_computation.4 | async-start | bytes 163840 | tf_op jit(solution)/shard_map/psum | solution.py:50
  15.0 104.8 %copy-start.10 = (s32[1,1,64]{2,1,0:T(1,128)S(1)}, s32[1,1,64]{2,1,0:T(1,128)}, u32[]{:S(2)}) copy-start(s32[1,1,64]{2,1,0:T(1,128)} %param.19) | copy-start | bytes 772
  15.0 117.6 %copy-start.7 = (f32[24,64]{1,0:T(8,128)S(1)}, f32[24,64]{1,0:T(8,128)}, u32[]{:S(2)}) copy-start(f32[24,64]{1,0:T(8,128)} %param.25) | copy-start | bytes 18436
  15.0 117.6 %copy-start.8 = (f32[24,64]{1,0:T(8,128)S(1)}, f32[24,64]{1,0:T(8,128)}, u32[]{:S(2)}) copy-start(f32[24,64]{1,0:T(8,128)} %param.20) | copy-start | bytes 18436
  15.0 117.6 %copy-start.9 = (f32[24,64]{1,0:T(8,128)S(1)}, f32[24,64]{1,0:T(8,128)}, u32[]{:S(2)}) copy-start(f32[24,64]{1,0:T(8,128)} %param.26) | copy-start | bytes 18436
  24.2 107.6 %reduce-scatter.13.cloned.1.call-start = ((), (), s32[]{:S(2)}) async-start(), calls=%async_computation.7 | async-start | bytes 98304
  120.6 113.4 %all-reduce.8.cloned.1.call-start = ((), (), s32[]{:S(2)}) async-start(), calls=%async_computation.5 | async-start | bytes 163840 | tf_op jit(solution)/shard_map/psum | solution.py:50
  137.8 157.7 %copy-start.2 = (f32[160,128]{1,0:T(8,128)S(1)}, f32[160,128]{1,0:T(8,128)}, u32[]{:S(2)}) copy-start(f32[160,128]{1,0:T(8,128)} %all-reduce.6.cloned.1.call-done) | copy-start | bytes 245764
  137.8 157.7 %copy-start.5 = (f32[160,128]{1,0:T(8,128)S(1)}, f32[160,128]{1,0:T(8,128)}, u32[]{:S(2)}) copy-start(f32[160,128]{1,0:T(8,128)} %param.24) | copy-start | bytes 245764
  137.8 157.7 %copy-start.6 = (f32[160,128]{1,0:T(8,128)S(1)}, f32[160,128]{1,0:T(8,128)}, u32[]{:S(2)}) copy-start(f32[160,128]{1,0:T(8,128)} %param.23) | copy-start | bytes 245764
  147.0 106.0 %reduce-scatter.15.cloned.1.call-start = ((), (), s32[]{:S(2)}) async-start(), calls=%async_computation.8 | async-start | bytes 98304
  234.0 61.5 %copy-start = (f32[160,128]{1,0:T(8,128)S(1)}, f32[160,128]{1,0:T(8,128)}, u32[]{:S(2)}) copy-start(f32[160,128]{1,0:T(8,128)} %all-reduce.8.cloned.1.call-done) | copy-start | bytes 245764
  241.9 71.7 %reduce-scatter.17.cloned.1.call-start = ((), (), s32[]{:S(2)}) async-start(), calls=%async_computation.9 | async-start | bytes 98304
  302.5 113.4 %all-reduce.10.cloned.1.call-start = ((), (), s32[]{:S(2)}) async-start(), calls=%async_computation.6 | async-start | bytes 163840 | tf_op jit(solution)/shard_map/psum | solution.py:50
  328.8 106.0 %reduce-scatter.19.cloned.1.call-start = ((), (), s32[]{:S(2)}) async-start(), calls=%async_computation.10 | async-start | bytes 98304
  415.8 61.9 %copy-start.1 = (f32[160,128]{1,0:T(8,128)S(1)}, f32[160,128]{1,0:T(8,128)}, u32[]{:S(2)}) copy-start(f32[160,128]{1,0:T(8,128)} %all-reduce.10.cloned.1.call-done) | copy-start | bytes 245764
Sparse Core Ops, SparseCore 0:
  24.3 88.5 all-reduce.5
  120.8 10.9 reduce-scatter.12
  147.1 86.8 all-reduce.7
  242.0 10.9 reduce-scatter.14
  302.6 10.9 reduce-scatter.16
  328.9 86.8 all-reduce.9
  423.8 10.9 reduce-scatter.18
where the time goes:
time: 486 us; the launch traced here: 485 us
  waiting for transfers between devices  305 us (63%)
  blocking collectives  93.6 us (19%)
  matrix products  52.1 us (11%)
  between operations  19 us (4%)
  local copies, waits for them, and re-layouts  9.73 us (2%)
  other arithmetic  5.46 us (1%)
    psum x3, waiting for transfers between devices, apply_forward(): return lax.psum(local_part, 'col')  262 us
    psum x2, blocking collectives, global_totals(): return lax.psum(stacked, ('row', 'col'))  79.3 us
    unnamed x11, waiting for transfers between devices  43.1 us
    dot_general x3, matrix products, forward_terms(): products = jnp.einsum('kij,kj->ki', flat_tiles, picked, precision=HIGH)  25 us
    dot_general x4, matrix products, apply_backward(): products = jnp.einsum('kij,ki->kj', flat_tiles, picked, precision=HIGH)  21.1 us
    all_gather x3, blocking collectives, apply_forward(): lax.all_gather(vector, 'row', axis=1, tiled=True)  14.4 us
  transfers between devices with their start and end apart: 7, of which 7 were waited for; matrix products, arithmetic and copies ran while one was open for 0% of the time, Pallas kernels for 0%

commit v1 on v0

--- a/solution.py
+++ b/solution.py
@@ -57,7 +57,7 @@
 
     def global_totals(values):
         stacked = jnp.stack([jnp.sum(value) for value in values])
-        return lax.psum(stacked, ("row", "col"))
+        return jnp.sum(lax.all_gather(stacked, ("row", "col")), axis=0)
 
     x_now, diag_now, linear_now = (x_start, cost_diag, linear)
     z_now, y_now = (z_start, y_start)

time: 486 us -> 491 us (1.010)
    psum x2 -> x0, blocking collectives: 79.3 us -> none  [global_totals(): return lax.psum(stacked, ('row', 'col'))]
    unnamed x0 -> x2, blocking collectives: none -> 78.7 us
where the time goes in v1:
time: 491 us; the launch traced here: 490 us
  waiting for transfers between devices  305 us (62%)
  blocking collectives  93.1 us (19%)
  matrix products  52.1 us (11%)
  between operations  19 us (4%)
  local copies, waits for them, and re-layouts  12.8 us (3%)
  other arithmetic  7.85 us (2%)
    psum x3, waiting for transfers between devices, apply_forward(): return lax.psum(local_part, 'col')  262 us
    unnamed x2, blocking collectives  78.7 us
    unnamed x11, waiting for transfers between devices  42.9 us
    dot_general x3, matrix products, forward_terms(): products = jnp.einsum('kij,kj->ki', flat_tiles, picked, precision=HIGH)  25 us
    dot_general x4, matrix products, apply_backward(): products = jnp.einsum('kij,ki->kj', flat_tiles, picked, precision=HIGH)  21.1 us
    all_gather x3, blocking collectives, apply_forward(): lax.all_gather(vector, 'row', axis=1, tiled=True)  14.4 us
  transfers between devices with their start and end apart: 7, of which 7 were waited for; matrix products, arithmetic and copies ran while one was open for 0% of the time, Pallas kernels for 0%

profile of v1, /device:TPU:0, one launch (start us, length us, event | category | flops | bytes accessed | tf_op | source)
XLA Modules:
  0.0 489.8 jit_solution(1402416280201542845)
XLA Ops:
  7.2 0.7 compare_select_fusion.1
  7.9 0.7 compare_and_fusion.1
  8.6 5.6 %all-gather = f32[2,64,24]{1,2,0:T(8,128)S(1)} all-gather(f32[1,64,24]{1,2,0:T(8,128)} %bitcast.126), channel_id=1, replica_groups=mesh['row'=2,'col'=16] {'row'}, dimensions={0}, use_global_device_ids=true | all-gather | bytes 18432 | tf_op jit(solution)/shard_map/all_gather | solution.py:49
  15.0 8.3 %fusion.12 = f32[64,1,128]{2,1,0:T(1,128)S(1)} fusion(f32[64,128,1]{1,2,0:T(1,128)S(1)} %bitcast.136, f32[1,1,64,128,128]{4,3,2,1,0:T(8,128)} %param.17), kind=kOutput, calls=%fused_computation.19 | convolution fusion | flops 12582912 | bytes 4259840 | tf_op jit(solution)/shard_map/kij,kj->ki/dot_general | solution.py:45
  23.3 0.8 fusion.16
  24.9 87.9 %all-reduce.10.cloned.1.call-done = f32[160,128]{1,0:T(8,128)} async-done(((f32[160,128]{1,0:T(8,128)}), f32[160,128]{1,0:T(8,128)}) %all-reduce.10.cloned.1.call-update) | async-done | bytes 81936 | tf_op jit(solution)/shard_map/psum | solution.py:50
  112.8 0.9 multiply_subtract_fusion.1
  114.4 5.3 %fusion.10 = f32[64,1,128]{2,1,0:T(1,128)S(1)} fusion(f32[64,128,1]{1,2,0:T(1,128)S(1)} %bitcast.137, f32[1,1,64,128,128]{4,3,2,1,0:T(8,128)} %param.17), kind=kOutput, calls=%fused_computation.17 | convolution fusion | flops 12582912 | bytes 4259840 | tf_op jit(solution)/shard_map/kij,ki->kj/dot_general | solution.py:54
  119.6 0.9 convolution_bitcast_fusion.3
  120.6 11.1 %reduce-scatter.13.cloned.1.call-done = f32[64,24]{1,0:T(8,128)} async-done(((f32[128,24]{1,0:T(8,128)}), f32[64,24]{1,0:T(8,128)}) %reduce-scatter.13.cloned.1.call-update) | async-done | bytes 6160
  131.7 0.8 copy.38
  132.5 4.4 all-gather.1
  137.7 8.4 %fusion.8 = f32[64,1,128]{2,1,0:T(1,128)S(1)} fusion(f32[64,128,1]{1,2,0:T(1,128)S(1)} %bitcast.138, f32[1,1,64,128,128]{4,3,2,1,0:T(8,128)} %param.17), kind=kOutput, calls=%fused_computation.15 | convolution fusion | flops 12582912 | bytes 4259840 | tf_op jit(solution)/shard_map/kij,kj->ki/dot_general | solution.py:45
  146.1 0.8 fusion.15
  147.0 87.0 %all-reduce.12.cloned.1.call-done = f32[160,128]{1,0:T(8,128)} async-done(((f32[160,128]{1,0:T(8,128)}), f32[160,128]{1,0:T(8,128)}) %all-reduce.12.cloned.1.call-update) | async-done | bytes 81936 | tf_op jit(solution)/shard_map/psum | solution.py:50
  234.0 1.6 gather_fusion.3
  235.6 5.3 %fusion.6 = f32[64,1,128]{2,1,0:T(1,128)S(1)} fusion(f32[64,128,1]{1,2,0:T(1,128)S(1)} %bitcast.139, f32[1,1,64,128,128]{4,3,2,1,0:T(8,128)} %param.17), kind=kOutput, calls=%fused_computation.13 | convolution fusion | flops 12582912 | bytes 4259840 | tf_op jit(solution)/shard_map/kij,ki->kj/dot_general | solution.py:54
  240.9 0.9 convolution_bitcast_fusion.2
  243.2 9.8 %reduce-scatter.15.cloned.1.call-done = f32[64,24]{1,0:T(8,128)} async-done(((f32[128,24]{1,0:T(8,128)}), f32[64,24]{1,0:T(8,128)}) %reduce-scatter.15.cloned.1.call-update) | async-done | bytes 6160
  252.9 0.8 copy.40
  253.8 0.6 multiply_reduce_fusion.2
  254.4 0.8 dynamic-update-slice
  255.1 0.8 dynamic-update-slice.1
  255.9 39.4 %all-reduce.5 = (f32[32]{0:T(128)S(1)}, f32[32]{0:T(128)S(1)}) all-reduce(f32[32]{0:T(128)S(1)} %dynamic-update-slice, f32[32]{0:T(128)S(1)} %dynamic-update-slice.1), channel_id=1, replica_groups=mesh['row'=2,'col'=16] {'row','col'}, use_global_device_ids=true, to_apply=%add | all-reduce | flops 64 | bytes 512
  295.3 0.6 reduce.4
  295.9 0.6 reduce.5
  298.0 0.6 gather_fusion.4
  298.7 5.3 %fusion.4 = f32[64,1,128]{2,1,0:T(1,128)S(1)} fusion(f32[64,128,1]{1,2,0:T(1,128)S(1)} %bitcast.140, f32[1,1,64,128,128]{4,3,2,1,0:T(8,128)} %param.17), kind=kOutput, calls=%fused_computation.11 | convolution fusion | flops 12582912 | bytes 4259840 | tf_op jit(solution)/shard_map/kij,ki->kj/dot_general | solution.py:54
  303.9 0.9 convolution_bitcast_fusion.1
  304.9 10.9 %reduce-scatter.17.cloned.1.call-done = f32[64,24]{1,0:T(8,128)} async-done(((f32[128,24]{1,0:T(8,128)}), f32[64,24]{1,0:T(8,128)}) %reduce-scatter.17.cloned.1.call-update) | async-done | bytes 6160
  315.8 0.8 copy.42
  316.6 4.4 all-gather.2
  321.8 8.3 %fusion.2 = f32[64,1,128]{2,1,0:T(1,128)S(1)} fusion(f32[64,128,1]{1,2,0:T(1,128)S(1)} %bitcast.134, f32[1,1,64,128,128]{4,3,2,1,0:T(8,128)} %param.17), kind=kOutput, calls=%fused_computation.9 | convolution fusion | flops 12582912 | bytes 4259840 | tf_op jit(solution)/shard_map/kij,kj->ki/dot_general | solution.py:45
  330.1 0.8 fusion.14
  331.0 86.9 %all-reduce.14.cloned.1.call-done = f32[160,128]{1,0:T(8,128)} async-done(((f32[160,128]{1,0:T(8,128)}), f32[160,128]{1,0:T(8,128)}) %all-reduce.14.cloned.1.call-update) | async-done | bytes 81936 | tf_op jit(solution)/shard_map/psum | solution.py:50
  418.0 1.6 gather_fusion.6
  419.6 5.3 %fusion = f32[64,1,128]{2,1,0:T(1,128)S(1)} fusion(f32[64,128,1]{1,2,0:T(1,128)S(1)} %bitcast.135, f32[1,1,64,128,128]{4,3,2,1,0:T(8,128)} %param.17), kind=kOutput, calls=%fused_computation.7 | convolution fusion | flops 12582912 | bytes 4259840 | tf_op jit(solution)/shard_map/kij,ki->kj/dot_general | solution.py:54
  424.9 0.9 convolution_bitcast_fusion
  425.8 11.1 %reduce-scatter.19.cloned.1.call-done = f32[64,24]{1,0:T(8,128)} async-done(((f32[128,24]{1,0:T(8,128)}), f32[64,24]{1,0:T(8,128)}) %reduce-scatter.19.cloned.1.call-update) | async-done | bytes 6160
  436.9 0.8 copy.44
  437.7 0.6 multiply_reduce_fusion
  438.3 0.8 dynamic-update-slice.2
  439.1 0.8 dynamic-update-slice.3
  439.8 39.3 %all-reduce.4 = (f32[32]{0:T(128)S(1)}, f32[32]{0:T(128)S(1)}) all-reduce(f32[32]{0:T(128)S(1)} %dynamic-update-slice.2, f32[32]{0:T(128)S(1)} %dynamic-update-slice.3), channel_id=1, replica_groups=mesh['row'=2,'col'=16] {'row','col'}, use_global_device_ids=true, to_apply=%add.2 | all-reduce | flops 64 | bytes 512
  479.1 0.6 reduce.6
  479.7 0.6 reduce.7
  481.6 0.6 multiply_add_fusion.5
  482.3 0.7 multiply_add_fusion
  (66 shorter events, 3.8 us)
Async XLA Ops:
  7.2 16.2 %copy-start.11 = (s32[1,1,64]{2,1,0:T(1,128)S(1)}, s32[1,1,64]{2,1,0:T(1,128)}, u32[]{:S(2)}) copy-start(s32[1,1,64]{2,1,0:T(1,128)} %param.18) | copy-start | bytes 772
  7.2 105.6 %copy-start.3 = (f32[160,128]{1,0:T(8,128)S(1)}, f32[160,128]{1,0:T(8,128)}, u32[]{:S(2)}) copy-start(f32[160,128]{1,0:T(8,128)} %param.22) | copy-start | bytes 245764
  7.2 105.6 %copy-start.4 = (f32[160,128]{1,0:T(8,128)S(1)}, f32[160,128]{1,0:T(8,128)}, u32[]{:S(2)}) copy-start(f32[160,128]{1,0:T(8,128)} %param.21) | copy-start | bytes 245764
  7.2 105.6 %all-reduce.10.cloned.1.call-start = ((), (), s32[]{:S(2)}) async-start(), calls=%async_computation.4 | async-start | bytes 163840 | tf_op jit(solution)/shard_map/psum | solution.py:50
  15.0 104.7 %copy-start.10 = (s32[1,1,64]{2,1,0:T(1,128)S(1)}, s32[1,1,64]{2,1,0:T(1,128)}, u32[]{:S(2)}) copy-start(s32[1,1,64]{2,1,0:T(1,128)} %param.19) | copy-start | bytes 772
  15.0 117.5 %copy-start.7 = (f32[24,64]{1,0:T(8,128)S(1)}, f32[24,64]{1,0:T(8,128)}, u32[]{:S(2)}) copy-start(f32[24,64]{1,0:T(8,128)} %param.25) | copy-start | bytes 18436
  15.0 117.5 %copy-start.8 = (f32[24,64]{1,0:T(8,128)S(1)}, f32[24,64]{1,0:T(8,128)}, u32[]{:S(2)}) copy-start(f32[24,64]{1,0:T(8,128)} %param.20) | copy-start | bytes 18436
  15.0 117.5 %copy-start.9 = (f32[24,64]{1,0:T(8,128)S(1)}, f32[24,64]{1,0:T(8,128)}, u32[]{:S(2)}) copy-start(f32[24,64]{1,0:T(8,128)} %param.26) | copy-start | bytes 18436
  24.2 107.5 %reduce-scatter.13.cloned.1.call-start = ((), (), s32[]{:S(2)}) async-start(), calls=%async_computation.7 | async-start | bytes 98304
  120.6 113.5 %all-reduce.12.cloned.1.call-start = ((), (), s32[]{:S(2)}) async-start(), calls=%async_computation.5 | async-start | bytes 163840 | tf_op jit(solution)/shard_map/psum | solution.py:50
  137.7 160.2 %copy-start.2 = (f32[160,128]{1,0:T(8,128)S(1)}, f32[160,128]{1,0:T(8,128)}, u32[]{:S(2)}) copy-start(f32[160,128]{1,0:T(8,128)} %all-reduce.10.cloned.1.call-done) | copy-start | bytes 245764
  137.7 160.2 %copy-start.5 = (f32[160,128]{1,0:T(8,128)S(1)}, f32[160,128]{1,0:T(8,128)}, u32[]{:S(2)}) copy-start(f32[160,128]{1,0:T(8,128)} %param.24) | copy-start | bytes 245764
  137.7 160.2 %copy-start.6 = (f32[160,128]{1,0:T(8,128)S(1)}, f32[160,128]{1,0:T(8,128)}, u32[]{:S(2)}) copy-start(f32[160,128]{1,0:T(8,128)} %param.23) | copy-start | bytes 245764
  146.9 106.0 %reduce-scatter.15.cloned.1.call-start = ((), (), s32[]{:S(2)}) async-start(), calls=%async_computation.8 | async-start | bytes 98304
  234.0 63.9 %copy-start = (f32[160,128]{1,0:T(8,128)S(1)}, f32[160,128]{1,0:T(8,128)}, u32[]{:S(2)}) copy-start(f32[160,128]{1,0:T(8,128)} %all-reduce.12.cloned.1.call-done) | copy-start | bytes 245764
  241.8 74.0 %reduce-scatter.17.cloned.1.call-start = ((), (), s32[]{:S(2)}) async-start(), calls=%async_computation.9 | async-start | bytes 98304
  304.9 113.1 %all-reduce.14.cloned.1.call-start = ((), (), s32[]{:S(2)}) async-start(), calls=%async_computation.6 | async-start | bytes 163840 | tf_op jit(solution)/shard_map/psum | solution.py:50
  331.0 105.9 %reduce-scatter.19.cloned.1.call-start = ((), (), s32[]{:S(2)}) async-start(), calls=%async_computation.10 | async-start | bytes 98304
  417.9 64.3 %copy-start.1 = (f32[160,128]{1,0:T(8,128)S(1)}, f32[160,128]{1,0:T(8,128)}, u32[]{:S(2)}) copy-start(f32[160,128]{1,0:T(8,128)} %all-reduce.14.cloned.1.call-done) | copy-start | bytes 245764
Sparse Core Ops, SparseCore 0:
  24.3 88.4 all-reduce.9
  120.7 10.9 reduce-scatter.12
  147.1 86.9 all-reduce.11
  242.0 10.9 reduce-scatter.14
  305.0 10.7 reduce-scatter.16
  331.1 86.8 all-reduce.13
  425.9 10.9 reduce-scatter.18
